TPU v7x, 256 devices: a whole 4x4x8 slice. The times are simulated.
256 devices in a mesh: seq: 16 (over z_lo, x), hid: 16 (over z_hi, y, core).
Axes of the slice: x: 4, y: 4, z: 8 (z_hi: 2, z_lo: 4; z = z_hi * 4 + z_lo), core: 2. Of those that a mesh axis runs over, the one named last changes fastest.
Arguments:
- tokens: bfloat16 [65536, 2048], P('seq', 'hid'), may hold values from -6 to 6
- cotangent: bfloat16 [65536, 2048], P('seq', 'hid'), may hold values from -6 to 6
- seq_first: bfloat16 [128, 512, 512], P('seq'), may hold values from -0.25 to 0.25
- seq_second: bfloat16 [512, 128, 128], P('seq'), may hold values from -0.5 to 0.5
- feat_first: bfloat16 [32, 64, 64], P('hid'), may hold values from -0.75 to 0.75
- feature_second_blocks: bfloat16 [64, 32, 32], P('hid'), may hold values from -1 to 1
- gate_scale: float32 [2048], P('hid'), may hold values from 0.5 to 2
- gate_bias: float32 [2048], P('hid'), may hold values from -3 to 3
Outputs:
- result: bfloat16 [65536, 2048], P('seq', 'hid')
- token_grad: bfloat16 [65536, 2048], P('seq', 'hid')
- first_grad: float32 [128, 512, 512], P('seq', 'hid')
- second_grad: float32 [512, 128, 128], P('seq', 'hid')
All inputs are finite; a program needn't handle non-finite values.
Results may differ from a plain program's by a relative error of at most 0.0061.
Values may be sent and summed in bfloat16 or wider, within the bound.
No kernel may reach another device: no remote copies, remote signals or barrier semaphores. Data moves between devices by JAX's collectives and lax.ppermute only.
A program may use at most 128 MiB of HBM per device.

v0:
```python
import jax
import jax.numpy as jnp
from jax import lax
from jax.sharding import Mesh
from jax.sharding import PartitionSpec as P

CHUNKS = 1
SEQ = ("zl", "x")
HID = ("zh", "y", "c")
PLANE = ("y", "c")
F32 = jnp.float32
BF16 = jnp.bfloat16


def swap(value, axes):
    return lax.all_to_all(value, axes, split_axis=0, concat_axis=0, tiled=True)


def gelu_slope(value):
    normal_cdf = 0.5 * (1.0 + jax.scipy.special.erf(value * 0.7071067811865476))
    density = jnp.exp(-0.5 * value * value) * 0.3989422804014327
    return normal_cdf + value * density


def dot(spec, left, right):
    return jnp.einsum(spec, left, right, preferred_element_type=F32)


def spread_second(blocks):
    group, panels = (blocks.shape[0], blocks.shape[1])
    width = group * panels
    rows = blocks.transpose(2, 0, 1).reshape(width, panels)
    col = lax.broadcasted_iota(jnp.int32, (panels, width), 1)
    pick = (col // group == lax.broadcasted_iota(jnp.int32, (panels, width), 0)).astype(BF16)
    full = dot("rb,bn->rn", rows, pick)
    at = lax.broadcasted_iota(jnp.int32, (width, width), 0) % group
    to = lax.broadcasted_iota(jnp.int32, (width, width), 1) % group
    return jnp.where(at == to, full, 0.0).astype(BF16)


def on_device(
    tokens,
    cotangent,
    seq_first,
    seq_second,
    feat_first,
    feature_second_blocks,
    gate_scale,
    gate_bias,
):
    n_seq, n_hid = (lax.axis_size(SEQ), lax.axis_size(HID))
    n_plane = lax.axis_size(PLANE)
    zh = lax.axis_index("zh")
    rows, width = tokens.shape
    blocks, block = (seq_first.shape[0], seq_first.shape[1])
    offs, nb = (seq_second.shape[0], seq_second.shape[1])
    groups, group = (feat_first.shape[0], feat_first.shape[1])
    per = offs // CHUNKS
    x_blocks = tokens.reshape(blocks, block, width)
    order = (n_seq, CHUNKS, per, blocks, width)
    x_rows = x_blocks.transpose(1, 0, 2).reshape(order)
    cot_rows = cotangent.reshape(blocks, block, width).transpose(1, 0, 2).reshape(order)
    second = seq_second.reshape(CHUNKS, per, nb, nb)
    eye = jnp.eye(groups, dtype=BF16)
    panel = (feat_first[:, :, None, :] * eye[:, None, :, None]).reshape(width, width)
    first = dot("qkj,qjc->kqc", seq_first, x_blocks).astype(BF16).reshape(order)
    x_plane = swap(x_blocks, PLANE).reshape(n_plane, block, width)
    spread = spread_second(lax.all_gather(feature_second_blocks, HID, axis=0, tiled=True))
    spread = spread.reshape(n_hid, width, n_hid, width)
    results, locals_, firsts, second_grads, first_grads = ([], [], [], [], [])
    for ch in range(CHUNKS):
        strided = swap(first[:, ch], SEQ).transpose(1, 0, 2, 3).reshape(per, nb, width)
        mixed_j = dot("jab,jbc->jac", second[ch], strided).astype(BF16)
        mixed_j = mixed_j.reshape(per, n_seq, blocks, width).transpose(1, 0, 2, 3)
        mixed = swap(mixed_j, SEQ).astype(F32)
        x_wide = x_rows[:, ch].astype(F32)
        cot = cot_rows[:, ch]
        gate = jax.nn.sigmoid(x_wide * gate_scale + gate_bias)
        hidden = (x_wide + gate * mixed).astype(BF16)
        inner = dot("sjqo,io->sjqi", hidden, panel).astype(BF16)
        by_row = (n_hid, per * blocks * n_seq // n_hid, width)
        cot_moved = swap(cot.reshape(by_row), HID)
        inner_moved = swap(inner.reshape(by_row), HID)
        inner_wide = inner_moved.astype(F32)
        act = jax.nn.gelu(inner_wide, approximate=False).astype(BF16)
        outer = dot("htc,hcdn->dtn", act, spread).astype(BF16)
        d_act = dot("dtn,hcdn->htc", cot_moved, spread)
        d_inner = (d_act * gelu_slope(inner_wide)).astype(BF16)
        d_back = swap(d_inner, HID).reshape(hidden.shape)
        d_hidden = cot.astype(F32) + dot("sjqi,io->sjqo", d_back, panel)
        d_mixed = (d_hidden * gate).astype(BF16)
        locals_.append(d_hidden * (1.0 + gate_scale * gate * (1.0 - gate) * mixed))
        d_mixed_j = swap(d_mixed, SEQ).transpose(1, 0, 2, 3).reshape(per, nb, width)
        d_first_j = dot("jab,jac->jbc", second[ch], d_mixed_j).astype(BF16)
        d_first_j = d_first_j.reshape(per, n_seq, blocks, width).transpose(1, 0, 2, 3)
        firsts.append(swap(d_first_j, SEQ))
        outer = swap(outer, HID).reshape(hidden.shape)
        results.append((hidden.astype(F32) + outer.astype(F32)).astype(BF16))
        part = dot("jac,jbc->jab", d_mixed_j, strided).astype(BF16)
        part = part.reshape(per, n_hid // n_plane, n_plane, nb // n_hid, nb)
        part = swap(part.transpose(2, 1, 0, 3, 4), PLANE)
        part = part.reshape(n_plane, n_hid // n_plane, per, nb // n_hid, nb).astype(F32).sum(0)
        keep = lax.dynamic_index_in_dim(part, zh, 0, keepdims=False)
        send = lax.dynamic_index_in_dim(part, 1 - zh, 0, keepdims=False)
        second_grads.append(keep + lax.ppermute(send, "zh", [(0, 1), (1, 0)]))
        d_first_q = firsts[ch].transpose(2, 0, 1, 3).reshape(blocks, n_seq * per, width)
        d_plane = swap(d_first_q, PLANE).reshape(n_plane, n_seq * per, width)
        prod = dot("skc,sjc->kj", d_plane, x_plane)
        prod = prod.reshape(n_hid // n_plane, n_plane, per, block)
        keep = lax.dynamic_index_in_dim(prod, zh, 0, keepdims=False)
        send = lax.dynamic_index_in_dim(prod, 1 - zh, 0, keepdims=False).astype(BF16)
        prod = keep + lax.ppermute(send, "zh", [(0, 1), (1, 0)]).astype(F32)
        first_grads.append(swap(prod, PLANE))

    def whole(parts):
        stacked = jnp.stack(parts, axis=1)
        return stacked.reshape(block, blocks, width).transpose(1, 0, 2).reshape(rows, width)

    d_first = jnp.stack(firsts, axis=1).reshape(block, blocks, width)
    seq_part = dot("qkj,kqc->qjc", seq_first, d_first).reshape(rows, width)
    token_grad = (seq_part + whole(locals_)).astype(BF16)
    first_grad = jnp.concatenate(first_grads, axis=1)
    second_grad = jnp.concatenate(second_grads, axis=0)
    return (whole(results), token_grad, first_grad, second_grad)


def solution(mesh):
    fine = Mesh(mesh.devices.reshape(4, 4, 2, 4, 2), ("zl", "x", "zh", "y", "c"))
    return jax.shard_map(
        on_device,
        mesh=fine,
        in_specs=(
            P(SEQ, HID),
            P(SEQ, HID),
            P(SEQ, None, None),
            P(SEQ, None, None),
            P(HID, None, None),
            P(HID, None, None),
            P(HID),
            P(HID),
        ),
        out_specs=(P(SEQ, HID), P(SEQ, HID), P(SEQ, HID, None), P(SEQ, HID, None)),
        check_vma=False,
    )
```

profile of v0, /device:TPU:32, one launch (start us, length us, event | category | flops | bytes accessed | tf_op | source)
XLA Modules:
  0.0 420.0 jit_solution(11952652844444209195)
XLA Ops:
  0.6 4.1 fusion.55
  5.5 34.3 %all_to_all.60 = bf16[16,32,8,128]{3,2,1,0:T(8,128)(2,1)S(1)} all-to-all(bf16[16,32,8,128]{3,2,1,0:T(8,128)(2,1)S(1)} %bitcast.158), channel_id=1, replica_groups=mesh['zl'=4,'x'=4,'zh'=2,'y'=4,'c'=2] {'zl','x'}, dimensions={0} | all-to-all | bytes 2097152 | tf_op jit(solution)/shard_map/all_to_all | solution.py:16
  41.5 5.1 %all-to-all-start.1 = ((bf16[16,32,8,128]{3,2,1,0:T(8,128)(2,1)}), bf16[16,32,8,128]{3,2,1,0:T(8,128)(2,1)}, u32[]{:S(2)}, u32[]{:S(2)}) async-start(bf16[16,32,8,128]{3,2,1,0:T(8,128)(2,1)} %bitcast.143), calls=%async_computation.1 | async-start | bytes 2097152 | tf_op jit(solution)/shard_map/all_to_all | solution.py:16
  46.6 3.0 copy.60
  49.7 22.0 %all-to-all-done.1 = bf16[16,32,8,128]{3,2,1,0:T(8,128)(2,1)} async-done(((bf16[16,32,8,128]{3,2,1,0:T(8,128)(2,1)}), bf16[16,32,8,128]{3,2,1,0:T(8,128)(2,1)}, u32[]{:S(2)}, u32[]{:S(2)}) %all-to-all-start.1) | async-done | bytes 1048608 | tf_op jit(solution)/shard_map/all_to_all | solution.py:16
  71.7 8.6 %all-to-all-start.4 = ((bf16[16,256,128]{2,1,0:T(8,128)(2,1)}), bf16[16,256,128]{2,1,0:T(8,128)(2,1)}, u32[]{:S(2)}, u32[]{:S(2)}) async-start(bf16[16,256,128]{2,1,0:T(8,128)(2,1)} %bitcast.154), calls=%async_computation.4 | async-start | bytes 2097152 | tf_op jit(solution)/shard_map/all_to_all | solution.py:16
  88.5 23.0 %all-to-all-done.4 = bf16[16,256,128]{2,1,0:T(8,128)(2,1)} async-done(((bf16[16,256,128]{2,1,0:T(8,128)(2,1)}), bf16[16,256,128]{2,1,0:T(8,128)(2,1)}, u32[]{:S(2)}, u32[]{:S(2)}) %all-to-all-start.4) | async-done | bytes 1048608 | tf_op jit(solution)/shard_map/all_to_all | solution.py:16
  111.6 4.3 %all-to-all-start.2 = ((bf16[16,256,128]{1,2,0:T(8,128)(2,1)}), bf16[16,256,128]{1,2,0:T(8,128)(2,1)}, u32[]{:S(2)}, u32[]{:S(2)}) async-start(bf16[16,256,128]{1,2,0:T(8,128)(2,1)} %copy.55), calls=%async_computation.2 | async-start | bytes 2097152 | tf_op jit(solution)/shard_map/all_to_all | solution.py:16
  115.9 40.7 %all_gather.3 = bf16[64,32,32]{2,1,0:T(8,128)(2,1)S(1)} all-gather(bf16[4,32,32]{2,1,0:T(8,128)(2,1)S(1)} %copy-done.10), channel_id=1, replica_groups=mesh['zl'=4,'x'=4,'zh'=2,'y'=4,'c'=2] {'zh','y','c'}, dimensions={0}, use_global_device_ids=true | all-gather | bytes 139264 | tf_op jit(solution)/shard_map/all_gather | solution.py:68
  157.5 5.2 %fusion.5 = bf16[256,8,16,128]{3,1,2,0:T(8,128)(2,1)} fusion(bf16[2048,32]{0,1:T(8,128)(2,1)S(1)} %reshape.92, s32[2048]{0:T(1024)S(1)} %get-tuple-element.7, s32[2048]{0:T(1024)S(1)} %get-tuple-element.8, pred[2048]{0:T(1024)(128)(4,1)S(1)} %get-tuple-element.11, s32[2048]{0:T(1024)S(1)} %get-tuple-element.6, s32[2048]{0:T(1024)S(1)} %get-tuple-element.9, ...), kind=kOutput, calls=%fused_computation.7 | convolution fusion | flops 289538048 | bytes 8556544 | tf_op jit(solution)/shard_map/rb,bn->rn/dot_general | solution.py:26
  162.7 9.8 %copy.82 = bf16[256,8,16,128]{3,2,1,0:T(8,128)(2,1)} copy(bf16[256,8,16,128]{3,1,2,0:T(8,128)(2,1)} %fusion.5) | data formatting | bytes 16777216
  172.5 8.1 %fusion.50 = bf16[16,256,128]{1,2,0:T(8,128)(2,1)S(1)} fusion(bf16[16,256,128]{1,2,0:T(8,128)(2,1)} %all-to-all-done.2, bf16[16,128,16,128]{1,0,3,2:T(8,128)(2,1)} %bitcast.151, bf16[16,256,128]{2,1,0:T(8,128)(2,1)} %all-to-all-done.4), kind=kOutput, calls=%fused_computation.69 | convolution fusion | flops 2153250816 | bytes 11534336 | tf_op jit(solution)/shard_map/dtn,hcdn->htc/dot_general | solution.py:26
  180.7 33.2 %all_to_all.61 = bf16[16,256,128]{1,2,0:T(8,128)(2,1)} all-to-all(bf16[16,256,128]{1,2,0:T(8,128)(2,1)S(1)} %fusion.50), channel_id=1, replica_groups=mesh['zl'=4,'x'=4,'zh'=2,'y'=4,'c'=2] {'zh','y','c'}, dimensions={0} | all-to-all | bytes 2097152 | tf_op jit(solution)/shard_map/all_to_all | solution.py:16
  216.2 4.8 %multiply_convert_fusion = (bf16[16,32,8,128]{3,2,1,0:T(8,128)(2,1)S(1)}, f32[16,32,8,128]{3,2,1,0:T(8,128)}) fusion(f32[128]{0:T(128)S(1)} %copy-done.11, f32[16,32,8,128]{3,2,1,0:T(8,128)} %bitcast.150, f32[128]{0:T(128)S(1)} %copy-done.12, bf16[16,32,8,128]{3,2,1,0:T(8,128)(2,1)} %all-to-all-done.1, bf16[128,128,1,1]{1,0,2,3:T(8,128)(2,1)S(1)} %reshape.106, ...), kind=kOutput, calls=%fused_computation.67 | convolution fusion | flops 142606336 | bytes 8422400 | tf_op jit(solution)/shard_map/sjqi,io->sjqo/dot_general | solution.py:26
  221.0 40.3 %all_to_all.62 = bf16[16,32,8,128]{3,2,1,0:T(8,128)(2,1)S(1)} all-to-all(bf16[16,32,8,128]{3,2,1,0:T(8,128)(2,1)S(1)} %get-tuple-element.4), channel_id=1, replica_groups=mesh['zl'=4,'x'=4,'zh'=2,'y'=4,'c'=2] {'zl','x'}, dimensions={0} | all-to-all | bytes 2097152 | tf_op jit(solution)/shard_map/all_to_all | solution.py:16
  261.3 4.3 %all-to-all-start.9 = ((bf16[8,512,128]{2,1,0:T(8,128)(2,1)}), bf16[8,512,128]{2,1,0:T(8,128)(2,1)}, u32[]{:S(2)}, u32[]{:S(2)}) async-start(bf16[8,512,128]{2,1,0:T(8,128)(2,1)} %bitcast.145), calls=%async_computation.9 | async-start | bytes 2097152 | tf_op jit(solution)/shard_map/all_to_all | solution.py:16
  267.4 14.1 %all-to-all-done.9 = bf16[8,512,128]{2,1,0:T(8,128)(2,1)} async-done(((bf16[8,512,128]{2,1,0:T(8,128)(2,1)}), bf16[8,512,128]{2,1,0:T(8,128)(2,1)}, u32[]{:S(2)}, u32[]{:S(2)}) %all-to-all-start.9) | async-done | bytes 1048608 | tf_op jit(solution)/shard_map/all_to_all | solution.py:16
  281.5 5.1 %all-to-all-start.7 = ((bf16[16,32,8,128]{3,2,1,0:T(8,128)(2,1)}), bf16[16,32,8,128]{3,2,1,0:T(8,128)(2,1)S(1)}, u32[]{:S(2)}, u32[]{:S(2)}) async-start(bf16[16,32,8,128]{3,2,1,0:T(8,128)(2,1)} %bitcast.157), calls=%async_computation.7 | async-start | bytes 2097152 | tf_op jit(solution)/shard_map/all_to_all | solution.py:16
  286.6 11.6 %fusion.59 = bf16[16,256,128]{1,2,0:T(8,128)(2,1)} fusion(bf16[16,128,16,128]{1,0,3,2:T(8,128)(2,1)} %bitcast.152, bf16[16,256,128]{1,2,0:T(8,128)(2,1)} %all-to-all-done.2), kind=kOutput, calls=%fused_computation.79 | convolution fusion | flops 2182610944 | bytes 10485760 | tf_op jit(solution)/shard_map/htc,hcdn->dtn/dot_general | solution.py:26
  298.2 13.8 %all-to-all-done.7 = bf16[16,32,8,128]{3,2,1,0:T(8,128)(2,1)S(1)} async-done(((bf16[16,32,8,128]{3,2,1,0:T(8,128)(2,1)}), bf16[16,32,8,128]{3,2,1,0:T(8,128)(2,1)S(1)}, u32[]{:S(2)}, u32[]{:S(2)}) %all-to-all-start.7) | async-done | bytes 1048608 | tf_op jit(solution)/shard_map/all_to_all | solution.py:16
  312.0 4.3 %all-to-all-start.3 = ((bf16[16,256,128]{1,2,0:T(8,128)(2,1)}), bf16[16,256,128]{1,2,0:T(8,128)(2,1)}, u32[]{:S(2)}, u32[]{:S(2)}) async-start(bf16[16,256,128]{1,2,0:T(8,128)(2,1)} %fusion.59), calls=%async_computation.3 | async-start | bytes 2097152 | tf_op jit(solution)/shard_map/all_to_all | solution.py:16
  317.6 30.1 %all-to-all-done.3 = bf16[16,256,128]{1,2,0:T(8,128)(2,1)} async-done(((bf16[16,256,128]{1,2,0:T(8,128)(2,1)}), bf16[16,256,128]{1,2,0:T(8,128)(2,1)}, u32[]{:S(2)}, u32[]{:S(2)}) %all-to-all-start.3) | async-done | bytes 1048608 | tf_op jit(solution)/shard_map/all_to_all | solution.py:16
  347.6 4.2 %all-to-all-start.8 = ((bf16[8,512,128]{2,1,0:T(8,128)(2,1)}), bf16[8,512,128]{2,1,0:T(8,128)(2,1)}, u32[]{:S(2)}, u32[]{:S(2)}) async-start(bf16[8,512,128]{2,1,0:T(8,128)(2,1)} %bitcast.156), calls=%async_computation.8 | async-start | bytes 2097152 | tf_op jit(solution)/shard_map/all_to_all | solution.py:16
  354.0 13.9 %all-to-all-done.8 = bf16[8,512,128]{2,1,0:T(8,128)(2,1)} async-done(((bf16[8,512,128]{2,1,0:T(8,128)(2,1)}), bf16[8,512,128]{2,1,0:T(8,128)(2,1)}, u32[]{:S(2)}, u32[]{:S(2)}) %all-to-all-start.8) | async-done | bytes 1048608 | tf_op jit(solution)/shard_map/all_to_all | solution.py:16
  367.8 3.6 all-to-all-start.11
  371.4 2.7 copy.58
  377.1 3.0 copy.67
  383.7 3.5 all-to-all-done.11
  389.4 11.9 %collective-permute-done = bf16[8,32,512]{2,1,0:T(8,128)(2,1)S(1)} collective-permute-done((bf16[8,32,512]{2,1,0:T(8,128)(2,1)}, bf16[8,32,512]{2,1,0:T(8,128)(2,1)S(1)}, u32[]{:S(2)}, u32[]{:S(2)}) %collective-permute-start) | collective-permute-done | bytes 262176 | tf_op jit(solution)/shard_map/ppermute | solution.py:112
  403.2 4.5 %all-to-all-start.10 = ((f32[8,32,512]{2,1,0:T(8,128)}), f32[8,32,512]{2,1,0:T(8,128)}, u32[]{:S(2)}, u32[]{:S(2)}) async-start(f32[8,32,512]{2,1,0:T(8,128)} %bitcast_add_fusion.2), calls=%async_computation.10 | async-start | bytes 1048576 | tf_op jit(solution)/shard_map/all_to_all | solution.py:16
  408.4 3.7 fusion.48
  413.4 4.7 %all-to-all-done.10 = f32[8,32,512]{2,1,0:T(8,128)} async-done(((f32[8,32,512]{2,1,0:T(8,128)}), f32[8,32,512]{2,1,0:T(8,128)}, u32[]{:S(2)}, u32[]{:S(2)}) %all-to-all-start.10) | async-done | bytes 524320 | tf_op jit(solution)/shard_map/all_to_all | solution.py:16
  (62 shorter events, 33.4 us)
Async XLA Ops:
  0.6 39.2 %copy-start = (bf16[32,128,128]{2,1,0:T(8,128)(2,1)S(1)}, bf16[32,128,128]{2,1,0:T(8,128)(2,1)}, u32[]{:S(2)}) copy-start(bf16[32,128,128]{2,1,0:T(8,128)(2,1)} %param.11) | copy-start | bytes 3145732
  41.5 30.2 %all-to-all-start.1 = ((bf16[16,32,8,128]{3,2,1,0:T(8,128)(2,1)}), bf16[16,32,8,128]{3,2,1,0:T(8,128)(2,1)}, u32[]{:S(2)}, u32[]{:S(2)}) async-start(bf16[16,32,8,128]{3,2,1,0:T(8,128)(2,1)} %bitcast.143), calls=%async_computation.1 | async-start | bytes 2097152 | tf_op jit(solution)/shard_map/all_to_all | solution.py:16
  46.6 33.6 %copy-start.2 = (bf16[4096,128]{1,0:T(8,128)(2,1)S(1)}, bf16[4096,128]{1,0:T(8,128)(2,1)}, u32[]{:S(2)}) copy-start(bf16[4096,128]{1,0:T(8,128)(2,1)} %param.8) | copy-start | bytes 3145732
  71.7 39.9 %all-to-all-start.4 = ((bf16[16,256,128]{2,1,0:T(8,128)(2,1)}), bf16[16,256,128]{2,1,0:T(8,128)(2,1)}, u32[]{:S(2)}, u32[]{:S(2)}) async-start(bf16[16,256,128]{2,1,0:T(8,128)(2,1)} %bitcast.154), calls=%async_computation.4 | async-start | bytes 2097152 | tf_op jit(solution)/shard_map/all_to_all | solution.py:16
  80.4 2.6 copy-start.9
  80.4 2.8 copy-start.11
  80.4 2.8 copy-start.12
  85.8 1.0 copy-start.3
  87.2 28.7 %copy-start.10 = (bf16[4,32,32]{2,1,0:T(8,128)(2,1)S(1)}, bf16[4,32,32]{2,1,0:T(8,128)(2,1)}, u32[]{:S(2)}) copy-start(bf16[4,32,32]{2,1,0:T(8,128)(2,1)} %param.13) | copy-start | bytes 24580
  111.6 61.0 %all-to-all-start.2 = ((bf16[16,256,128]{1,2,0:T(8,128)(2,1)}), bf16[16,256,128]{1,2,0:T(8,128)(2,1)}, u32[]{:S(2)}, u32[]{:S(2)}) async-start(bf16[16,256,128]{1,2,0:T(8,128)(2,1)} %copy.55), calls=%async_computation.2 | async-start | bytes 2097152 | tf_op jit(solution)/shard_map/all_to_all | solution.py:16
  180.7 35.5 %copy-start.7 = (bf16[8,512,128]{2,0,1:T(8,128)(2,1)S(1)}, bf16[8,512,128]{2,0,1:T(8,128)(2,1)}, u32[]{:S(2)}) copy-start(bf16[8,512,128]{2,0,1:T(8,128)(2,1)} %copy.60) | copy-start | bytes 3145732
  261.3 20.2 %all-to-all-start.9 = ((bf16[8,512,128]{2,1,0:T(8,128)(2,1)}), bf16[8,512,128]{2,1,0:T(8,128)(2,1)}, u32[]{:S(2)}, u32[]{:S(2)}) async-start(bf16[8,512,128]{2,1,0:T(8,128)(2,1)} %bitcast.145), calls=%async_computation.9 | async-start | bytes 2097152 | tf_op jit(solution)/shard_map/all_to_all | solution.py:16
  281.5 30.5 %all-to-all-start.7 = ((bf16[16,32,8,128]{3,2,1,0:T(8,128)(2,1)}), bf16[16,32,8,128]{3,2,1,0:T(8,128)(2,1)S(1)}, u32[]{:S(2)}, u32[]{:S(2)}) async-start(bf16[16,32,8,128]{3,2,1,0:T(8,128)(2,1)} %bitcast.157), calls=%async_computation.7 | async-start | bytes 2097152 | tf_op jit(solution)/shard_map/all_to_all | solution.py:16
  312.0 5.5 %copy-start.5 = (bf16[16,32,8,128]{3,2,1,0:T(8,128)(2,1)}, bf16[16,32,8,128]{3,2,1,0:T(8,128)(2,1)S(1)}, u32[]{:S(2)}) copy-start(bf16[16,32,8,128]{3,2,1,0:T(8,128)(2,1)S(1)} %all-to-all-done.7) | copy-start | bytes 3145732
  312.0 35.6 %all-to-all-start.3 = ((bf16[16,256,128]{1,2,0:T(8,128)(2,1)}), bf16[16,256,128]{1,2,0:T(8,128)(2,1)}, u32[]{:S(2)}, u32[]{:S(2)}) async-start(bf16[16,256,128]{1,2,0:T(8,128)(2,1)} %fusion.59), calls=%async_computation.3 | async-start | bytes 2097152 | tf_op jit(solution)/shard_map/all_to_all | solution.py:16
  347.6 20.2 %all-to-all-start.8 = ((bf16[8,512,128]{2,1,0:T(8,128)(2,1)}), bf16[8,512,128]{2,1,0:T(8,128)(2,1)}, u32[]{:S(2)}, u32[]{:S(2)}) async-start(bf16[8,512,128]{2,1,0:T(8,128)(2,1)} %bitcast.156), calls=%async_computation.8 | async-start | bytes 2097152 | tf_op jit(solution)/shard_map/all_to_all | solution.py:16
  367.8 19.4 %all-to-all-start.11 = ((bf16[8,2,32,8,128]{4,3,1,2,0:T(8,128)(2,1)}), bf16[8,2,32,8,128]{4,3,1,2,0:T(8,128)(2,1)S(1)}, u32[]{:S(2)}, u32[]{:S(2)}) async-start(bf16[8,2,32,8,128]{4,3,1,2,0:T(8,128)(2,1)} %bitcast.141), calls=%async_computation.11 | async-start | bytes 2097152 | tf_op jit(solution)/shard_map/all_to_all | solution.py:16
  371.4 2.7 copy-start.4
  382.4 1.4 copy-start.8
  383.2 25.2 %copy-start.6 = (bf16[16,32,8,128]{3,2,1,0:T(8,128)(2,1)S(1)}, bf16[16,32,8,128]{3,2,1,0:T(8,128)(2,1)}, u32[]{:S(2)}) copy-start(bf16[16,32,8,128]{3,2,1,0:T(8,128)(2,1)} %copy-done.5) | copy-start | bytes 3145732
  383.2 18.1 %collective-permute-start = (bf16[8,32,512]{2,1,0:T(8,128)(2,1)}, bf16[8,32,512]{2,1,0:T(8,128)(2,1)S(1)}, u32[]{:S(2)}, u32[]{:S(2)}) collective-permute-start(bf16[8,32,512]{2,1,0:T(8,128)(2,1)} %fusion.105), channel_id=1, source_target_pairs={{0,8},{8,0},{1,9},{9,1},{2,10},{10,2},{3,11},{11,3},{4,12},{12,4},... | collective-permute-start | bytes 786440 | tf_op jit(solution)/shard_map/ppermute | solution.py:112
  387.4 20.3 %collective-permute-start.1 = (f32[32,8,128]{2,1,0:T(8,128)S(1)}, f32[32,8,128]{2,1,0:T(8,128)S(1)}, u32[]{:S(2)}, u32[]{:S(2)}) collective-permute-start(f32[32,8,128]{2,1,0:T(8,128)S(1)} %dynamic-slice_bitcast_fusion), channel_id=1, source_target_pairs={{0,8},{8,0},{1,9},{9,1},{2,10},{10,2},{3,11},{11,3},{4,12},{12,4},... | collective-permute-start | bytes 393224 | tf_op jit(solution)/shard_map/ppermute | solution.py:105
  403.2 14.9 %all-to-all-start.10 = ((f32[8,32,512]{2,1,0:T(8,128)}), f32[8,32,512]{2,1,0:T(8,128)}, u32[]{:S(2)}, u32[]{:S(2)}) async-start(f32[8,32,512]{2,1,0:T(8,128)} %bitcast_add_fusion.2), calls=%async_computation.10 | async-start | bytes 1048576 | tf_op jit(solution)/shard_map/all_to_all | solution.py:16
  408.4 11.6 %copy-start.1 = (bf16[32,128,128]{2,1,0:T(8,128)(2,1)S(1)}, bf16[32,128,128]{2,1,0:T(8,128)(2,1)}, u32[]{:S(2)}) copy-start(bf16[32,128,128]{2,1,0:T(8,128)(2,1)} %param.11) | copy-start | bytes 3145732
where the time goes:
time: 421 us; the launch traced here: 420 us
  blocking collectives  148 us (35%)
  waiting for transfers between devices  137 us (33%)
  starting transfers between devices  46.5 us (11%)
  matrix products  42.2 us (10%)
  local copies, waits for them, and re-layouts  37.5 us (9%)
  other arithmetic  7.41 us (2%)
    all_to_all x9, waiting for transfers between devices, swap(): return lax.all_to_all(value, axes, split_axis=0, concat_axis=0, tiled=True)  125 us
    all_to_all x3, blocking collectives, swap(): return lax.all_to_all(value, axes, split_axis=0, concat_axis=0, tiled=True)  108 us
    all_to_all x9, starting transfers between devices, swap(): return lax.all_to_all(value, axes, split_axis=0, concat_axis=0, tiled=True)  44 us
    dot_general x11, matrix products, dot(): return jnp.einsum(spec, left, right, preferred_element_type=F32)  42.2 us
    all_gather x1, blocking collectives, on_device(): lax.all_gather(feature_second_blocks, HID, axis=0, tiled=True)  40.7 us
    unnamed x28, local copies, waits for them, and re-layouts  12.7 us
    ppermute x1, waiting for transfers between devices, on_device(): prod = keep + lax.ppermute(send, 'zh', [(0, 1), (1, 0)]).astype(F32)  11.9 us
  transfers between devices with their start and end apart: 11, of which 9 were waited for; matrix products, arithmetic and copies ran while one was open for 15% of the time, Pallas kernels for 0%

commit v1 on v0

--- a/solution.py
+++ b/solution.py
@@ -65,7 +65,12 @@
     panel = (feat_first[:, :, None, :] * eye[:, None, :, None]).reshape(width, width)
     first = dot("qkj,qjc->kqc", seq_first, x_blocks).astype(BF16).reshape(order)
     x_plane = swap(x_blocks, PLANE).reshape(n_plane, block, width)
-    spread = spread_second(lax.all_gather(feature_second_blocks, HID, axis=0, tiled=True))
+    spread = spread_second(
+        jnp.concatenate(
+            lax.all_to_all(jnp.stack([feature_second_blocks] * lax.axis_size(HID)), HID, 0, 0),
+            axis=0,
+        )
+    )
     spread = spread.reshape(n_hid, width, n_hid, width)
     results, locals_, firsts, second_grads, first_grads = ([], [], [], [], [])
     for ch in range(CHUNKS):

time: 421 us -> 401 us (0.952)
  blocking collectives: 148 us -> 65.1 us
  waiting for transfers between devices: 137 us -> 184 us
  starting transfers between devices: 46.5 us -> 59.8 us
    all_to_all x3 -> x2, blocking collectives: 108 us -> 65.1 us  [swap(): return lax.all_to_all(value, axes, split_axis=0, concat_axis=0, tiled=True)]
    all_gather x1 -> x0, blocking collectives: 40.7 us -> none  [on_device(): lax.all_gather(feature_second_blocks, HID, axis=0, tiled=True)]
    all_to_all x9 -> x10, waiting for transfers between devices: 125 us -> 163 us  [swap(): return lax.all_to_all(value, axes, split_axis=0, concat_axis=0, tiled=True)]
    all_to_all x0 -> x1, waiting for transfers between devices: none -> 9.87 us  [on_device(): lax.all_to_all(jnp.stack([feature_second_blocks] * lax.axis_size(HID)), H...]
    all_to_all x0 -> x1, starting transfers between devices: none -> 8.5 us  [on_device(): lax.all_to_all(jnp.stack([feature_second_blocks] * lax.axis_size(HID)), H...]
    all_to_all x9 -> x10, starting transfers between devices: 44 us -> 48.7 us  [swap(): return lax.all_to_all(value, axes, split_axis=0, concat_axis=0, tiled=True)]
    unnamed x28 -> x30, local copies, waits for them, and re-layouts: 12.7 us -> 14.2 us
  transfers between devices with their start and end apart: 11 -> 13, of which waited for: 9 -> 12; matrix products, arithmetic and copies ran while one was open for 15% -> 16% of each run, Pallas kernels for 0% -> 0%
where the time goes in v1:
time: 401 us; the launch traced here: 399 us
  waiting for transfers between devices  184 us (46%)
  blocking collectives  65.1 us (16%)
  starting transfers between devices  59.8 us (15%)
  matrix products  42.2 us (11%)
  local copies, waits for them, and re-layouts  39.7 us (10%)
  other arithmetic  7.41 us (2%)
    all_to_all x10, waiting for transfers between devices, swap(): return lax.all_to_all(value, axes, split_axis=0, concat_axis=0, tiled=True)  163 us
    all_to_all x2, blocking collectives, swap(): return lax.all_to_all(value, axes, split_axis=0, concat_axis=0, tiled=True)  65.1 us
    all_to_all x10, starting transfers between devices, swap(): return lax.all_to_all(value, axes, split_axis=0, concat_axis=0, tiled=True)  48.7 us
    dot_general x11, matrix products, dot(): return jnp.einsum(spec, left, right, preferred_element_type=F32)  42.2 us
    unnamed x30, local copies, waits for them, and re-layouts  14.2 us
    ppermute x1, waiting for transfers between devices, on_device(): prod = keep + lax.ppermute(send, 'zh', [(0, 1), (1, 0)]).astype(F32)  11.9 us
    all_to_all x1, waiting for transfers between devices, on_device(): lax.all_to_all(jnp.stack([feature_second_blocks] * lax.axis_size(HID)), H...  9.87 us
    all_to_all x1, starting transfers between devices, on_device(): lax.all_to_all(jnp.stack([feature_second_blocks] * lax.axis_size(HID)), H...  8.5 us
  transfers between devices with their start and end apart: 13, of which 12 were waited for; matrix products, arithmetic and copies ran while one was open for 16% of the time, Pallas kernels for 0%

profile of v1, /device:TPU:32, one launch (start us, length us, event | category | flops | bytes accessed | tf_op | source)
XLA Modules:
  0.0 399.5 jit_solution(6285050712112846602)
XLA Ops:
  0.6 4.1 %fusion.55 = bf16[512,8,128]{0,2,1:T(8,128)(2,1)S(1)} fusion(bf16[8,512,128]{2,1,0:T(8,128)(2,1)} %bitcast.146, bf16[8,512,512]{2,1,0:T(8,128)(2,1)} %param.10), kind=kOutput, calls=%fused_computation.75 | convolution fusion | flops 537395200 | bytes 6291456 | tf_op jit(solution)/shard_map/qkj,qjc->kqc/dot_general | solution.py:26
  6.2 8.5 %all-to-all-start = ((bf16[16,32,8,128]{3,2,1,0:T(8,128)(2,1)}), bf16[16,32,8,128]{3,2,1,0:T(8,128)(2,1)S(1)}, u32[]{:S(2)}, u32[]{:S(2)}) async-start(bf16[16,32,8,128]{3,2,1,0:T(8,128)(2,1)} %bitcast.4), calls=%async_computation | async-start | bytes 2097152 | tf_op jit(solution)/shard_map/all_to_all | solution.py:16
  16.0 24.4 %all-to-all-done = bf16[16,32,8,128]{3,2,1,0:T(8,128)(2,1)S(1)} async-done(((bf16[16,32,8,128]{3,2,1,0:T(8,128)(2,1)}), bf16[16,32,8,128]{3,2,1,0:T(8,128)(2,1)S(1)}, u32[]{:S(2)}, u32[]{:S(2)}) %all-to-all-start) | async-done | bytes 1048608 | tf_op jit(solution)/shard_map/all_to_all | solution.py:16
  40.4 8.5 %all-to-all-start.2 = ((bf16[16,2,2048]{2,1,0:T(2,128)(2,1)}), bf16[16,2,2048]{2,1,0:T(2,128)(2,1)S(1)}, u32[]{:S(2)}, u32[]{:S(2)}) async-start(bf16[16,2,2048]{2,1,0:T(2,128)(2,1)} %reshape.119), calls=%async_computation.2 | async-start | bytes 262144 | tf_op jit(solution)/shard_map/all_to_all | solution.py:70
  50.6 9.9 %all-to-all-done.2 = bf16[16,2,2048]{2,1,0:T(2,128)(2,1)S(1)} async-done(((bf16[16,2,2048]{2,1,0:T(2,128)(2,1)}), bf16[16,2,2048]{2,1,0:T(2,128)(2,1)S(1)}, u32[]{:S(2)}, u32[]{:S(2)}) %all-to-all-start.2) | async-done | bytes 131104 | tf_op jit(solution)/shard_map/all_to_all | solution.py:70
  60.5 5.3 %all-to-all-start.1 = ((bf16[16,32,8,128]{3,2,1,0:T(8,128)(2,1)}), bf16[16,32,8,128]{3,2,1,0:T(8,128)(2,1)}, u32[]{:S(2)}, u32[]{:S(2)}) async-start(bf16[16,32,8,128]{3,2,1,0:T(8,128)(2,1)} %bitcast.145), calls=%async_computation.1 | async-start | bytes 2097152 | tf_op jit(solution)/shard_map/all_to_all | solution.py:16
  68.9 22.8 %all-to-all-done.1 = bf16[16,32,8,128]{3,2,1,0:T(8,128)(2,1)} async-done(((bf16[16,32,8,128]{3,2,1,0:T(8,128)(2,1)}), bf16[16,32,8,128]{3,2,1,0:T(8,128)(2,1)}, u32[]{:S(2)}, u32[]{:S(2)}) %all-to-all-start.1) | async-done | bytes 1048608 | tf_op jit(solution)/shard_map/all_to_all | solution.py:16
  91.7 4.4 %all-to-all-start.5 = ((bf16[16,256,128]{2,1,0:T(8,128)(2,1)}), bf16[16,256,128]{2,1,0:T(8,128)(2,1)}, u32[]{:S(2)}, u32[]{:S(2)}) async-start(bf16[16,256,128]{2,1,0:T(8,128)(2,1)} %bitcast.156), calls=%async_computation.5 | async-start | bytes 2097152 | tf_op jit(solution)/shard_map/all_to_all | solution.py:16
  104.4 22.9 %all-to-all-done.5 = bf16[16,256,128]{2,1,0:T(8,128)(2,1)} async-done(((bf16[16,256,128]{2,1,0:T(8,128)(2,1)}), bf16[16,256,128]{2,1,0:T(8,128)(2,1)}, u32[]{:S(2)}, u32[]{:S(2)}) %all-to-all-start.5) | async-done | bytes 1048608 | tf_op jit(solution)/shard_map/all_to_all | solution.py:16
  127.3 4.5 %all-to-all-start.3 = ((bf16[16,256,128]{1,2,0:T(8,128)(2,1)}), bf16[16,256,128]{1,2,0:T(8,128)(2,1)}, u32[]{:S(2)}, u32[]{:S(2)}) async-start(bf16[16,256,128]{1,2,0:T(8,128)(2,1)} %copy.76), calls=%async_computation.3 | async-start | bytes 2097152 | tf_op jit(solution)/shard_map/all_to_all | solution.py:16
  133.0 5.2 %fusion.5 = bf16[256,8,16,128]{3,1,2,0:T(8,128)(2,1)} fusion(bf16[2048,32]{0,1:T(8,128)(2,1)S(1)} %reshape.98, s32[2048]{0:T(1024)S(1)} %get-tuple-element.7, s32[2048]{0:T(1024)S(1)} %get-tuple-element.8, pred[2048]{0:T(1024)(128)(4,1)S(1)} %get-tuple-element.11, s32[2048]{0:T(1024)S(1)} %get-tuple-element.6, s32[2048]{0:T(1024)S(1)} %get-tuple-element.9, ...), kind=kOutput, calls=%fused_computation.7 | convolution fusion | flops 289538048 | bytes 8556544 | tf_op jit(solution)/shard_map/rb,bn->rn/dot_general | solution.py:26
  138.2 9.8 %copy.103 = bf16[256,8,16,128]{3,2,1,0:T(8,128)(2,1)} copy(bf16[256,8,16,128]{3,1,2,0:T(8,128)(2,1)} %fusion.5) | data formatting | bytes 16777216
  148.0 12.3 %all-to-all-done.3 = bf16[16,256,128]{1,2,0:T(8,128)(2,1)} async-done(((bf16[16,256,128]{1,2,0:T(8,128)(2,1)}), bf16[16,256,128]{1,2,0:T(8,128)(2,1)}, u32[]{:S(2)}, u32[]{:S(2)}) %all-to-all-start.3) | async-done | bytes 1048608 | tf_op jit(solution)/shard_map/all_to_all | solution.py:16
  160.4 8.1 %fusion.50 = bf16[16,256,128]{1,2,0:T(8,128)(2,1)S(1)} fusion(bf16[16,256,128]{1,2,0:T(8,128)(2,1)} %all-to-all-done.3, bf16[16,128,16,128]{1,0,3,2:T(8,128)(2,1)} %bitcast.153, bf16[16,256,128]{2,1,0:T(8,128)(2,1)} %all-to-all-done.5), kind=kOutput, calls=%fused_computation.69 | convolution fusion | flops 2153250816 | bytes 11534336 | tf_op jit(solution)/shard_map/dtn,hcdn->htc/dot_general | solution.py:26
  168.5 33.0 %all_to_all.65 = bf16[16,256,128]{1,2,0:T(8,128)(2,1)} all-to-all(bf16[16,256,128]{1,2,0:T(8,128)(2,1)S(1)} %fusion.50), channel_id=1, replica_groups=mesh['zl'=4,'x'=4,'zh'=2,'y'=4,'c'=2] {'zh','y','c'}, dimensions={0} | all-to-all | bytes 2097152 | tf_op jit(solution)/shard_map/all_to_all | solution.py:16
  203.7 4.9 %multiply_convert_fusion = (bf16[16,32,8,128]{3,2,1,0:T(8,128)(2,1)S(1)}, f32[16,32,8,128]{3,2,1,0:T(8,128)}) fusion(f32[128]{0:T(128)S(1)} %copy-done.11, f32[16,32,8,128]{3,2,1,0:T(8,128)} %bitcast.152, f32[128]{0:T(128)S(1)} %copy-done.12, bf16[16,32,8,128]{3,2,1,0:T(8,128)(2,1)} %all-to-all-done.1, bf16[128,128,1,1]{1,0,2,3:T(8,128)(2,1)S(1)} %reshape.112, ...), kind=kOutput, calls=%fused_computation.67 | convolution fusion | flops 142606336 | bytes 8422400 | tf_op jit(solution)/shard_map/sjqi,io->sjqo/dot_general | solution.py:26
  208.6 32.2 %all_to_all.66 = bf16[16,32,8,128]{3,2,1,0:T(8,128)(2,1)S(1)} all-to-all(bf16[16,32,8,128]{3,2,1,0:T(8,128)(2,1)S(1)} %get-tuple-element.4), channel_id=1, replica_groups=mesh['zl'=4,'x'=4,'zh'=2,'y'=4,'c'=2] {'zl','x'}, dimensions={0} | all-to-all | bytes 2097152 | tf_op jit(solution)/shard_map/all_to_all | solution.py:16
  240.8 4.3 %all-to-all-start.10 = ((bf16[8,512,128]{2,1,0:T(8,128)(2,1)}), bf16[8,512,128]{2,1,0:T(8,128)(2,1)}, u32[]{:S(2)}, u32[]{:S(2)}) async-start(bf16[8,512,128]{2,1,0:T(8,128)(2,1)} %bitcast.147), calls=%async_computation.10 | async-start | bytes 2097152 | tf_op jit(solution)/shard_map/all_to_all | solution.py:16
  246.9 14.1 %all-to-all-done.10 = bf16[8,512,128]{2,1,0:T(8,128)(2,1)} async-done(((bf16[8,512,128]{2,1,0:T(8,128)(2,1)}), bf16[8,512,128]{2,1,0:T(8,128)(2,1)}, u32[]{:S(2)}, u32[]{:S(2)}) %all-to-all-start.10) | async-done | bytes 1048608 | tf_op jit(solution)/shard_map/all_to_all | solution.py:16
  261.0 5.1 %all-to-all-start.8 = ((bf16[16,32,8,128]{3,2,1,0:T(8,128)(2,1)}), bf16[16,32,8,128]{3,2,1,0:T(8,128)(2,1)S(1)}, u32[]{:S(2)}, u32[]{:S(2)}) async-start(bf16[16,32,8,128]{3,2,1,0:T(8,128)(2,1)} %bitcast.159), calls=%async_computation.8 | async-start | bytes 2097152 | tf_op jit(solution)/shard_map/all_to_all | solution.py:16
  266.1 11.6 %fusion.59 = bf16[16,256,128]{1,2,0:T(8,128)(2,1)} fusion(bf16[16,128,16,128]{1,0,3,2:T(8,128)(2,1)} %bitcast.154, bf16[16,256,128]{1,2,0:T(8,128)(2,1)} %all-to-all-done.3), kind=kOutput, calls=%fused_computation.79 | convolution fusion | flops 2182610944 | bytes 10485760 | tf_op jit(solution)/shard_map/htc,hcdn->dtn/dot_general | solution.py:26
  277.7 13.8 %all-to-all-done.8 = bf16[16,32,8,128]{3,2,1,0:T(8,128)(2,1)S(1)} async-done(((bf16[16,32,8,128]{3,2,1,0:T(8,128)(2,1)}), bf16[16,32,8,128]{3,2,1,0:T(8,128)(2,1)S(1)}, u32[]{:S(2)}, u32[]{:S(2)}) %all-to-all-start.8) | async-done | bytes 1048608 | tf_op jit(solution)/shard_map/all_to_all | solution.py:16
  291.5 4.4 %all-to-all-start.4 = ((bf16[16,256,128]{1,2,0:T(8,128)(2,1)}), bf16[16,256,128]{1,2,0:T(8,128)(2,1)}, u32[]{:S(2)}, u32[]{:S(2)}) async-start(bf16[16,256,128]{1,2,0:T(8,128)(2,1)} %fusion.59), calls=%async_computation.4 | async-start | bytes 2097152 | tf_op jit(solution)/shard_map/all_to_all | solution.py:16
  297.0 30.1 %all-to-all-done.4 = bf16[16,256,128]{1,2,0:T(8,128)(2,1)} async-done(((bf16[16,256,128]{1,2,0:T(8,128)(2,1)}), bf16[16,256,128]{1,2,0:T(8,128)(2,1)}, u32[]{:S(2)}, u32[]{:S(2)}) %all-to-all-start.4) | async-done | bytes 1048608 | tf_op jit(solution)/shard_map/all_to_all | solution.py:16
  327.1 4.2 %all-to-all-start.9 = ((bf16[8,512,128]{2,1,0:T(8,128)(2,1)}), bf16[8,512,128]{2,1,0:T(8,128)(2,1)}, u32[]{:S(2)}, u32[]{:S(2)}) async-start(bf16[8,512,128]{2,1,0:T(8,128)(2,1)} %bitcast.158), calls=%async_computation.9 | async-start | bytes 2097152 | tf_op jit(solution)/shard_map/all_to_all | solution.py:16
  333.4 13.9 %all-to-all-done.9 = bf16[8,512,128]{2,1,0:T(8,128)(2,1)} async-done(((bf16[8,512,128]{2,1,0:T(8,128)(2,1)}), bf16[8,512,128]{2,1,0:T(8,128)(2,1)}, u32[]{:S(2)}, u32[]{:S(2)}) %all-to-all-start.9) | async-done | bytes 1048608 | tf_op jit(solution)/shard_map/all_to_all | solution.py:16
  347.3 3.6 all-to-all-start.12
  363.2 3.5 all-to-all-done.12
  368.9 11.9 %collective-permute-done = bf16[8,32,512]{2,1,0:T(8,128)(2,1)S(1)} collective-permute-done((bf16[8,32,512]{2,1,0:T(8,128)(2,1)}, bf16[8,32,512]{2,1,0:T(8,128)(2,1)S(1)}, u32[]{:S(2)}, u32[]{:S(2)}) %collective-permute-start) | collective-permute-done | bytes 262176 | tf_op jit(solution)/shard_map/ppermute | solution.py:117
  382.7 4.5 %all-to-all-start.11 = ((f32[8,32,512]{2,1,0:T(8,128)}), f32[8,32,512]{2,1,0:T(8,128)}, u32[]{:S(2)}, u32[]{:S(2)}) async-start(f32[8,32,512]{2,1,0:T(8,128)} %bitcast_add_fusion.2), calls=%async_computation.11 | async-start | bytes 1048576 | tf_op jit(solution)/shard_map/all_to_all | solution.py:16
  387.9 3.7 fusion.48
  392.9 4.7 %all-to-all-done.11 = f32[8,32,512]{2,1,0:T(8,128)} async-done(((f32[8,32,512]{2,1,0:T(8,128)}), f32[8,32,512]{2,1,0:T(8,128)}, u32[]{:S(2)}, u32[]{:S(2)}) %all-to-all-start.11) | async-done | bytes 524320 | tf_op jit(solution)/shard_map/all_to_all | solution.py:16
  (67 shorter events, 44.3 us)
Async XLA Ops:
  0.6 48.3 %copy-start = (bf16[32,128,128]{2,1,0:T(8,128)(2,1)S(1)}, bf16[32,128,128]{2,1,0:T(8,128)(2,1)}, u32[]{:S(2)}) copy-start(bf16[32,128,128]{2,1,0:T(8,128)(2,1)} %param.11) | copy-start | bytes 3145732
  4.8 10.0 %copy-start.9 = (bf16[4,32,32]{2,1,0:T(8,128)(2,1)S(1)}, bf16[4,32,32]{2,1,0:T(8,128)(2,1)}, u32[]{:S(2)}) copy-start(bf16[4,32,32]{2,1,0:T(8,128)(2,1)} %param.13) | copy-start | bytes 24580
  6.2 34.2 %all-to-all-start = ((bf16[16,32,8,128]{3,2,1,0:T(8,128)(2,1)}), bf16[16,32,8,128]{3,2,1,0:T(8,128)(2,1)S(1)}, u32[]{:S(2)}, u32[]{:S(2)}) async-start(bf16[16,32,8,128]{3,2,1,0:T(8,128)(2,1)} %bitcast.4), calls=%async_computation | async-start | bytes 2097152 | tf_op jit(solution)/shard_map/all_to_all | solution.py:16
  40.4 20.1 %all-to-all-start.2 = ((bf16[16,2,2048]{2,1,0:T(2,128)(2,1)}), bf16[16,2,2048]{2,1,0:T(2,128)(2,1)S(1)}, u32[]{:S(2)}, u32[]{:S(2)}) async-start(bf16[16,2,2048]{2,1,0:T(2,128)(2,1)} %reshape.119), calls=%async_computation.2 | async-start | bytes 262144 | tf_op jit(solution)/shard_map/all_to_all | solution.py:70
  60.5 31.2 %all-to-all-start.1 = ((bf16[16,32,8,128]{3,2,1,0:T(8,128)(2,1)}), bf16[16,32,8,128]{3,2,1,0:T(8,128)(2,1)}, u32[]{:S(2)}, u32[]{:S(2)}) async-start(bf16[16,32,8,128]{3,2,1,0:T(8,128)(2,1)} %bitcast.145), calls=%async_computation.1 | async-start | bytes 2097152 | tf_op jit(solution)/shard_map/all_to_all | solution.py:16
  65.8 30.2 %copy-start.2 = (bf16[4096,128]{1,0:T(8,128)(2,1)S(1)}, bf16[4096,128]{1,0:T(8,128)(2,1)}, u32[]{:S(2)}) copy-start(bf16[4096,128]{1,0:T(8,128)(2,1)} %param.8) | copy-start | bytes 3145732
  91.7 35.6 %all-to-all-start.5 = ((bf16[16,256,128]{2,1,0:T(8,128)(2,1)}), bf16[16,256,128]{2,1,0:T(8,128)(2,1)}, u32[]{:S(2)}, u32[]{:S(2)}) async-start(bf16[16,256,128]{2,1,0:T(8,128)(2,1)} %bitcast.156), calls=%async_computation.5 | async-start | bytes 2097152 | tf_op jit(solution)/shard_map/all_to_all | solution.py:16
  96.2 2.6 copy-start.10
  96.2 2.8 copy-start.11
  96.2 2.8 copy-start.12
  101.6 1.0 copy-start.3
  127.3 33.1 %all-to-all-start.3 = ((bf16[16,256,128]{1,2,0:T(8,128)(2,1)}), bf16[16,256,128]{1,2,0:T(8,128)(2,1)}, u32[]{:S(2)}, u32[]{:S(2)}) async-start(bf16[16,256,128]{1,2,0:T(8,128)(2,1)} %copy.76), calls=%async_computation.3 | async-start | bytes 2097152 | tf_op jit(solution)/shard_map/all_to_all | solution.py:16
  168.5 35.2 %copy-start.7 = (bf16[8,512,128]{2,0,1:T(8,128)(2,1)S(1)}, bf16[8,512,128]{2,0,1:T(8,128)(2,1)}, u32[]{:S(2)}) copy-start(bf16[8,512,128]{2,0,1:T(8,128)(2,1)} %copy.81) | copy-start | bytes 3145732
  240.8 20.2 %all-to-all-start.10 = ((bf16[8,512,128]{2,1,0:T(8,128)(2,1)}), bf16[8,512,128]{2,1,0:T(8,128)(2,1)}, u32[]{:S(2)}, u32[]{:S(2)}) async-start(bf16[8,512,128]{2,1,0:T(8,128)(2,1)} %bitcast.147), calls=%async_computation.10 | async-start | bytes 2097152 | tf_op jit(solution)/shard_map/all_to_all | solution.py:16
  261.0 30.5 %all-to-all-start.8 = ((bf16[16,32,8,128]{3,2,1,0:T(8,128)(2,1)}), bf16[16,32,8,128]{3,2,1,0:T(8,128)(2,1)S(1)}, u32[]{:S(2)}, u32[]{:S(2)}) async-start(bf16[16,32,8,128]{3,2,1,0:T(8,128)(2,1)} %bitcast.159), calls=%async_computation.8 | async-start | bytes 2097152 | tf_op jit(solution)/shard_map/all_to_all | solution.py:16
  291.5 5.5 %copy-start.5 = (bf16[16,32,8,128]{3,2,1,0:T(8,128)(2,1)}, bf16[16,32,8,128]{3,2,1,0:T(8,128)(2,1)S(1)}, u32[]{:S(2)}) copy-start(bf16[16,32,8,128]{3,2,1,0:T(8,128)(2,1)S(1)} %all-to-all-done.8) | copy-start | bytes 3145732
  291.5 35.6 %all-to-all-start.4 = ((bf16[16,256,128]{1,2,0:T(8,128)(2,1)}), bf16[16,256,128]{1,2,0:T(8,128)(2,1)}, u32[]{:S(2)}, u32[]{:S(2)}) async-start(bf16[16,256,128]{1,2,0:T(8,128)(2,1)} %fusion.59), calls=%async_computation.4 | async-start | bytes 2097152 | tf_op jit(solution)/shard_map/all_to_all | solution.py:16
  327.1 20.2 %all-to-all-start.9 = ((bf16[8,512,128]{2,1,0:T(8,128)(2,1)}), bf16[8,512,128]{2,1,0:T(8,128)(2,1)}, u32[]{:S(2)}, u32[]{:S(2)}) async-start(bf16[8,512,128]{2,1,0:T(8,128)(2,1)} %bitcast.158), calls=%async_computation.9 | async-start | bytes 2097152 | tf_op jit(solution)/shard_map/all_to_all | solution.py:16
  347.3 19.4 %all-to-all-start.12 = ((bf16[8,2,32,8,128]{4,3,1,2,0:T(8,128)(2,1)}), bf16[8,2,32,8,128]{4,3,1,2,0:T(8,128)(2,1)S(1)}, u32[]{:S(2)}, u32[]{:S(2)}) async-start(bf16[8,2,32,8,128]{4,3,1,2,0:T(8,128)(2,1)} %bitcast.143), calls=%async_computation.12 | async-start | bytes 2097152 | tf_op jit(solution)/shard_map/all_to_all | solution.py:16
  350.9 2.7 copy-start.4
  361.9 1.4 copy-start.8
  362.7 25.2 %copy-start.6 = (bf16[16,32,8,128]{3,2,1,0:T(8,128)(2,1)S(1)}, bf16[16,32,8,128]{3,2,1,0:T(8,128)(2,1)}, u32[]{:S(2)}) copy-start(bf16[16,32,8,128]{3,2,1,0:T(8,128)(2,1)} %copy-done.5) | copy-start | bytes 3145732
  362.7 18.1 %collective-permute-start = (bf16[8,32,512]{2,1,0:T(8,128)(2,1)}, bf16[8,32,512]{2,1,0:T(8,128)(2,1)S(1)}, u32[]{:S(2)}, u32[]{:S(2)}) collective-permute-start(bf16[8,32,512]{2,1,0:T(8,128)(2,1)} %fusion.105), channel_id=1, source_target_pairs={{0,8},{8,0},{1,9},{9,1},{2,10},{10,2},{3,11},{11,3},{4,12},{12,4},... | collective-permute-start | bytes 786440 | tf_op jit(solution)/shard_map/ppermute | solution.py:117
  366.9 20.3 %collective-permute-start.1 = (f32[32,8,128]{2,1,0:T(8,128)S(1)}, f32[32,8,128]{2,1,0:T(8,128)S(1)}, u32[]{:S(2)}, u32[]{:S(2)}) collective-permute-start(f32[32,8,128]{2,1,0:T(8,128)S(1)} %dynamic-slice_bitcast_fusion), channel_id=1, source_target_pairs={{0,8},{8,0},{1,9},{9,1},{2,10},{10,2},{3,11},{11,3},{4,12},{12,4},... | collective-permute-start | bytes 393224 | tf_op jit(solution)/shard_map/ppermute | solution.py:110
  382.7 14.9 %all-to-all-start.11 = ((f32[8,32,512]{2,1,0:T(8,128)}), f32[8,32,512]{2,1,0:T(8,128)}, u32[]{:S(2)}, u32[]{:S(2)}) async-start(f32[8,32,512]{2,1,0:T(8,128)} %bitcast_add_fusion.2), calls=%async_computation.11 | async-start | bytes 1048576 | tf_op jit(solution)/shard_map/all_to_all | solution.py:16
  387.9 11.6 %copy-start.1 = (bf16[32,128,128]{2,1,0:T(8,128)(2,1)S(1)}, bf16[32,128,128]{2,1,0:T(8,128)(2,1)}, u32[]{:S(2)}) copy-start(bf16[32,128,128]{2,1,0:T(8,128)(2,1)} %param.11) | copy-start | bytes 3145732
